TPU v7x, 32 devices: a whole 2x2x4 slice. The times are simulated.
32 devices in a mesh: path: 2 (over x), mesh: 2 (over y), grid: 8 (over z, core).
Axes of the slice: x: 2, y: 2, z: 4, core: 2. Of those that a mesh axis runs over, the one named last changes fastest.
Arguments:
- path_bands: float32 [2, 16, 64, 64, 128], P('path', None, 'grid'), may hold values from -6 to 6
- occupied: float32 [2, 1, 64, 64, 128], P('mesh', None, 'grid', 'path'), may hold values from -6 to 6
- path_kpts: int32 [2, 3], P('path'), may hold values from 0 to 7
- mesh_kpts: int32 [2, 3], replicated, may hold values from 0 to 7
- mesh_shift: int32 [2, 3], replicated, may hold values from -1 to 1
Outputs:
- applied: float32 [2, 16, 64, 64, 128], P('path', 'mesh', 'grid')
- intersection: float32 [2, 2, 16, 16], P('path')
All inputs are finite; a program needn't handle non-finite values.
Results may differ from a plain program's by a relative error of at most 0.0001.
Values sent between devices are 32-bit elements; how exact they have to be, the bound alone decides.
No kernel may reach another device: no remote copies, remote signals or barrier semaphores. Data moves between devices by JAX's collectives and lax.ppermute only.
A program may use at most 64 MiB of HBM per device.

v0:
```python
import math
import jax
import jax.numpy as jnp
from jax import lax
from jax.sharding import PartitionSpec as P

KDIV = 8
BOX_LENGTH = 42.7
SCREEN_SQ = 0.04
MIXING = 0.25
HIGHEST_PRECISION = lax.Precision.HIGHEST


def signed_frequencies(indices, points):
    return (indices + points // 2) % points - points // 2


def dft_tables(positions, points):
    freqs = jnp.arange(points, dtype=jnp.int32)
    product = positions[:, None] * freqs[None, :] % points
    angles = 2.0 * math.pi / points * product.astype(jnp.float32)
    return (jnp.cos(angles), jnp.sin(angles))


def last_matrix(points, inverse):
    cosine_table, sine_table = dft_tables(jnp.arange(points, dtype=jnp.int32), points)
    if inverse:
        upper = jnp.concatenate([cosine_table, sine_table], 1)
        lower = jnp.concatenate([-sine_table, cosine_table], 1)
    else:
        upper = jnp.concatenate([cosine_table, -sine_table], 1)
        lower = jnp.concatenate([sine_table, cosine_table], 1)
    return jnp.concatenate([upper, lower], 0)


def along_axis(values, cosine_table, sine_table, contract_dim, inverse):
    letters = "abcde"
    form = (
        letters
        + ","
        + letters[contract_dim]
        + "w->"
        + letters[:contract_dim]
        + "w"
        + letters[contract_dim + 1 :]
    )
    cos_part = jnp.einsum(form, values, cosine_table, precision=HIGHEST_PRECISION)
    sin_part = jnp.einsum(form, values, sine_table, precision=HIGHEST_PRECISION)
    half_width = values.shape[-1] // 2
    sin_real = sin_part[..., :half_width]
    sin_imag = sin_part[..., half_width:]
    if inverse:
        return cos_part + jnp.concatenate([-sin_imag, sin_real], -1)
    return cos_part + jnp.concatenate([sin_imag, -sin_real], -1)


def rotate_orbitals(orbitals, shifts, x_planes):
    points = orbitals.shape[3]
    coords = jnp.arange(points, dtype=jnp.int32)
    product = (
        shifts[:, 0][:, None, None, None] * x_planes[None, :, None, None]
        + shifts[:, 1][:, None, None, None] * coords[None, None, :, None]
        + shifts[:, 2][:, None, None, None] * coords[None, None, None, :]
    ) % points
    angles = 2.0 * math.pi / points * product.astype(jnp.float32)
    cosines = jnp.cos(angles)[:, None]
    sines = jnp.sin(angles)[:, None]
    real_part = orbitals[..., :points]
    imag_part = orbitals[..., points:]
    return jnp.concatenate(
        [real_part * cosines - imag_part * sines, real_part * sines + imag_part * cosines], -1
    )


def pair_fields(rotated, band_fields):
    points = band_fields.shape[2]
    rot_real = rotated[..., :points][:, :, None]
    rot_imag = rotated[..., points:][:, :, None]
    band_real = band_fields[..., :points][None, None]
    band_imag = band_fields[..., points:][None, None]
    pairs = jnp.concatenate(
        [rot_real * band_real + rot_imag * band_imag, rot_real * band_imag - rot_imag * band_real],
        -1,
    )
    return pairs.reshape(
        (rotated.shape[0], rotated.shape[1] * band_fields.shape[0]) + band_fields.shape[1:]
    )


def accumulate(rotated, potential, nbands):
    points = rotated.shape[3]
    shaped = potential.reshape((rotated.shape[0], rotated.shape[1], nbands) + potential.shape[2:])
    rot_real = rotated[..., :points][:, :, None]
    rot_imag = rotated[..., points:][:, :, None]
    pot_real = shaped[..., :points]
    pot_imag = shaped[..., points:]
    summed = jnp.concatenate(
        [
            jnp.sum(rot_real * pot_real - rot_imag * pot_imag, axis=(0, 1)),
            jnp.sum(rot_real * pot_imag + rot_imag * pot_real, axis=(0, 1)),
        ],
        -1,
    )
    return -MIXING * summed


def intersection_part(band_fields, applied):
    points = band_fields.shape[2]
    nbands = band_fields.shape[0]
    band_real = band_fields[..., :points].reshape(nbands, -1)
    band_imag = band_fields[..., points:].reshape(nbands, -1)
    app_real = applied[..., :points].reshape(applied.shape[0], -1)
    app_imag = applied[..., points:].reshape(applied.shape[0], -1)
    real_sum = jnp.dot(band_real, app_real.T, precision=HIGHEST_PRECISION) + jnp.dot(
        band_imag, app_imag.T, precision=HIGHEST_PRECISION
    )
    imag_sum = jnp.dot(band_real, app_imag.T, precision=HIGHEST_PRECISION) - jnp.dot(
        band_imag, app_real.T, precision=HIGHEST_PRECISION
    )
    return jnp.stack([real_sum, imag_sum]) / float(points**3)


def screened_kernel(path_point, mesh_points, y_rows, points):
    offset_frac = (path_point[None, :] - mesh_points).astype(jnp.float32) / KDIV
    all_freqs = signed_frequencies(jnp.arange(points, dtype=jnp.int32), points).astype(jnp.float32)
    row_freqs = signed_frequencies(y_rows, points).astype(jnp.float32)
    square_x = (all_freqs[None, :] + offset_frac[:, 0:1]) ** 2
    square_y = (row_freqs[None, :] + offset_frac[:, 1:2]) ** 2
    square_z = (all_freqs[None, :] + offset_frac[:, 2:3]) ** 2
    squares = square_x[:, :, None, None] + square_y[:, None, :, None] + square_z[:, None, None, :]
    kernel = (
        4.0 * math.pi / ((2.0 * math.pi / BOX_LENGTH) ** 2 * squares + SCREEN_SQ) / float(points**3)
    )
    return jnp.concatenate([kernel, kernel], -1)


def per_device(path_bands, occupied, path_kpts, mesh_kpts, mesh_shift):
    points = path_bands.shape[3]
    nbands = path_bands.shape[1]
    local_planes = path_bands.shape[2]
    grid_count = lax.axis_size("grid")
    mesh_count = lax.axis_size("mesh")
    grid_index = lax.axis_index("grid")
    mesh_index = lax.axis_index("mesh")
    whole_orbitals = lax.all_gather(occupied, "path", axis=3, tiled=True)
    forward_z = last_matrix(points, False)
    inverse_z = last_matrix(points, True)
    cos_y, sin_y = dft_tables(jnp.arange(points, dtype=jnp.int32), points)
    band_all = path_bands[0]
    path_point = path_kpts[0]
    share_planes = local_planes // mesh_count
    both_orbitals = lax.all_to_all(whole_orbitals, "mesh", split_axis=2, concat_axis=0, tiled=True)
    x_planes = (
        grid_index * local_planes
        + mesh_index * share_planes
        + jnp.arange(share_planes, dtype=jnp.int32)
    )
    rotated = rotate_orbitals(both_orbitals, mesh_shift, x_planes)
    band_mine = lax.dynamic_slice_in_dim(band_all, mesh_index * share_planes, share_planes, 1)
    values = pair_fields(rotated, band_mine)
    values = jnp.matmul(values, forward_z, precision=HIGHEST_PRECISION)
    pair_field = along_axis(values, cos_y, sin_y, 3, False)
    wide_count = mesh_count * grid_count
    rows_y = points // wide_count
    flat_index = mesh_index * grid_count + grid_index
    y_rows = flat_index * rows_y + jnp.arange(rows_y, dtype=jnp.int32)
    kernel = screened_kernel(path_point, mesh_kpts, y_rows, points)
    positions = jnp.arange(points, dtype=jnp.int32)
    piece_index = positions // share_planes
    plane_index = (
        piece_index % grid_count * local_planes
        + piece_index // grid_count * share_planes
        + positions % share_planes
    )
    cos_x, sin_x = dft_tables(plane_index, points)
    moved = (
        along_axis(
            lax.all_to_all(pair_field, ("mesh", "grid"), split_axis=3, concat_axis=2, tiled=True),
            cos_x,
            sin_x,
            2,
            False,
        )
        * kernel[:, None]
    )
    moved = along_axis(moved, cos_x.T, sin_x.T, 2, True)
    potential = lax.all_to_all(moved, ("mesh", "grid"), split_axis=2, concat_axis=3, tiled=True)
    values = potential
    values = along_axis(values, cos_y, sin_y, 3, True)
    applied = accumulate(
        rotated, jnp.matmul(values, inverse_z, precision=HIGHEST_PRECISION), nbands
    )
    partial_value = intersection_part(band_mine, applied)
    result_bands = lax.all_to_all(applied, "mesh", split_axis=0, concat_axis=1, tiled=True)
    intersection = lax.psum(partial_value, ("mesh", "grid"))
    return (result_bands[None], intersection[None])


def solution(mesh):
    return jax.shard_map(
        per_device,
        mesh=mesh,
        in_specs=(
            P("path", None, "grid", None, None),
            P("mesh", None, "grid", "path", None),
            P("path", None),
            P(),
            P(),
        ),
        out_specs=(P("path", "mesh", "grid", None, None), P("path", None, None, None)),
        check_vma=False,
    )
```

profile of v0, /device:TPU:0, one launch (start us, length us, event | category | flops | bytes accessed | tf_op | source)
XLA Modules:
  0.0 395.5 jit_solution(9331506577557012715)
XLA Ops:
  0.6 9.0 %all_gather.3 = f32[1,1,8,64,128]{4,3,1,0,2:T(8,128)} all-gather(f32[1,1,8,32,128]{4,3,1,0,2:T(8,128)} %bitcast.138), channel_id=1, replica_groups=mesh['path'=2,'mesh'=2,'grid'=8] {'path'}, dimensions={3}, use_global_device_ids=true | all-gather | bytes 393216 | tf_op jit(solution)/shard_map/all_gather | solution.py:145
  9.6 3.4 all-to-all-start
  14.1 1.7 constant_dynamic-slice_fusion
  18.1 2.0 copy.20
  20.1 2.0 copy.21
  23.9 3.4 multiply_add_fusion
  27.3 4.0 %fusion = f32[2,16,4,64,128]{4,3,2,1,0:T(8,128)S(1)} fusion(f32[2,1,16,4,64,64]{5,4,3,2,0,1:T(8,128)S(1)} %get-tuple-element.11, f32[2,1,16,4,64,64]{5,4,3,2,0,1:T(8,128)S(1)} %get-tuple-element.10, f32[64,64]{1,0:T(8,128)S(1)} %get-tuple-element.29, f32[64,64]{1,0:T(8,128)S(1)} %get-tuple-element.28, f32[64,64]{1,0:T(8,128)S(1)} %fusion.88), kind=kOutput, calls=%fused_computation.5 | convolution fusion | flops 1611710464 | bytes 8437760 | tf_op jit(solution)/shard_map/dot_general | solution.py:161
  31.3 4.2 %convolution_bitcast_fusion.3 = f32[2,16,4,64,128]{4,3,2,1,0:T(8,128)S(1)} fusion(f32[2,16,4,64,128]{4,3,2,1,0:T(8,128)S(1)} %fusion), kind=kOutput, calls=%fused_computation.25 | convolution fusion | flops 805363712 | bytes 8388608 | tf_op jit(solution)/shard_map/abcde,dw->abcwe/dot_general | solution.py:48
  35.5 1.9 fusion.139
  37.4 19.3 %maximum_add_fusion = f32[2,16,4,64,128]{4,3,2,1,0:T(8,128)S(1)} fusion(f32[2,16,4,64,64]{4,3,2,1,0:T(8,128)S(1)} %get-tuple-element.19, f32[2,16,4,64,64]{4,3,2,1,0:T(8,128)S(1)} %get-tuple-element.18, f32[2,16,4,64,128]{4,3,2,1,0:T(8,128)S(1)} %fusion), kind=kOutput, calls=%fused_computation.8 | convolution fusion | flops 807460864 | bytes 12582912 | tf_op jit(solution)/shard_map/abcde,dw->abcwe/dot_general | solution.py:47
  56.6 4.7 %copy.24 = f32[2,16,4,64,128]{4,2,1,0,3:T(4,128)} copy(f32[2,16,4,64,128]{4,3,2,1,0:T(8,128)S(1)} %maximum_add_fusion) | data formatting | bytes 8388608 | tf_op jit(solution)/shard_map/add | solution.py:54
  61.3 6.6 %all-to-all-start.1 = ((f32[2,16,4,64,128]{4,2,1,0,3:T(4,128)}), f32[2,16,4,64,128]{4,2,1,0,3:T(4,128)}, u32[]{:S(2)}, u32[]{:S(2)}) async-start(f32[2,16,4,64,128]{4,2,1,0,3:T(4,128)} %copy.24), calls=%async_computation.1 | async-start | bytes 8388608 | tf_op jit(solution)/shard_map/all_to_all | solution.py:178
  68.7 87.0 %all-to-all-done.1 = f32[2,16,4,64,128]{4,2,1,0,3:T(4,128)} async-done(((f32[2,16,4,64,128]{4,2,1,0,3:T(4,128)}), f32[2,16,4,64,128]{4,2,1,0,3:T(4,128)}, u32[]{:S(2)}, u32[]{:S(2)}) %all-to-all-start.1) | async-done | bytes 4194336 | tf_op jit(solution)/shard_map/all_to_all | solution.py:178
  155.7 3.4 copy.25
  159.1 4.2 %convolution_bitcast_fusion.2 = f32[2,16,64,4,128]{4,2,3,1,0:T(8,128)S(1)} fusion(f32[2,16,64,4,128]{4,2,3,1,0:T(8,128)S(1)} %bitcast.131, s32[64]{0:T(128)S(1)} %fusion.91), kind=kOutput, calls=%fused_computation.24 | convolution fusion | flops 805363712 | bytes 8388864 | tf_op jit(solution)/shard_map/abcde,cw->abwde/dot_general | solution.py:48
  163.3 1.9 fusion.138
  165.2 6.8 %fusion.3 = f32[2,16,64,4,128]{4,2,3,1,0:T(8,128)S(1)} fusion(f32[2,16,64,4,64]{4,2,3,1,0:T(8,128)S(1)} %get-tuple-element.17, f32[2,16,64,4,64]{4,2,3,1,0:T(8,128)S(1)} %get-tuple-element.16, f32[2,16,64,4,128]{4,2,3,1,0:T(8,128)S(1)} %bitcast.132, f32[2,64,4,128]{3,1,2,0:T(8,128)S(1)} %pad_maximum_fusion, s32[64]{0:T(128)S(1)} %fusion.91), kind=kOutput, calls=%fused_computation.10 | convolution fusion | flops 808509440 | bytes 12845312 | tf_op jit(solution)/shard_map/abcde,cw->abwde/dot_general | solution.py:47
  172.0 4.3 %convolution_bitcast_fusion.1 = f32[2,16,64,4,128]{4,2,3,1,0:T(8,128)S(1)} fusion(f32[2,16,64,4,128]{4,2,3,1,0:T(8,128)S(1)} %fusion.3, s32[64]{0:T(128)S(1)} %fusion.91), kind=kOutput, calls=%fused_computation.23 | convolution fusion | flops 805363712 | bytes 8388864 | tf_op jit(solution)/shard_map/abcde,cw->abwde/dot_general | solution.py:48
  178.0 6.3 %maximum_add_fusion.2 = f32[2,16,64,4,128]{4,2,3,1,0:T(8,128)S(1)} fusion(f32[2,16,64,4,64]{4,2,3,1,0:T(8,128)S(1)} %get-tuple-element.15, f32[2,16,64,4,64]{4,2,3,1,0:T(8,128)S(1)} %get-tuple-element.14, f32[2,16,64,4,128]{4,2,3,1,0:T(8,128)S(1)} %fusion.3, s32[64]{0:T(128)S(1)} %fusion.91), kind=kOutput, calls=%fused_computation.11 | convolution fusion | flops 807460864 | bytes 12583168 | tf_op jit(solution)/shard_map/abcde,cw->abwde/dot_general | solution.py:47
  184.3 2.9 copy.28
  187.2 101.4 %all_to_all.63 = f32[2,16,64,4,128]{4,3,1,0,2:T(4,128)S(1)} all-to-all(f32[2,16,64,4,128]{4,3,1,0,2:T(4,128)S(1)} %copy.28), channel_id=1, replica_groups=mesh['path'=2,'mesh'=2,'grid'=8] {'mesh','grid'}, dimensions={2} | all-to-all | bytes 8388608 | tf_op jit(solution)/shard_map/all_to_all | solution.py:187
  289.8 4.2 %convolution_bitcast_fusion = f32[2,16,4,64,128]{4,3,2,1,0:T(8,128)S(1)} fusion(f32[2,16,4,64,128]{4,3,2,1,0:T(8,128)S(1)} %bitcast.133), kind=kOutput, calls=%fused_computation.22 | convolution fusion | flops 805363712 | bytes 8388608 | tf_op jit(solution)/shard_map/abcde,dw->abcwe/dot_general | solution.py:48
  294.0 4.2 %fusion.65 = f32[64,2,16,4,128]{4,0,3,2,1:T(8,128)S(1)} fusion(f32[2,16,4,64,128]{4,3,2,1,0:T(8,128)S(1)} %bitcast.134), kind=kOutput, calls=%fused_computation.85 | convolution fusion | flops 805363712 | bytes 8388608 | tf_op jit(solution)/shard_map/abcde,dw->abcwe/dot_general | solution.py:47
  299.9 4.2 %fusion.8 = f32[2,1,16,4,64,128]{5,4,3,2,0,1:T(8,128)S(1)} fusion(f32[2,16,4,64,64]{4,3,2,1,0:T(8,128)S(1)} %get-tuple-element.13, f32[2,16,4,64,64]{4,3,2,1,0:T(8,128)S(1)} %get-tuple-element.12, f32[64,2,16,4,128]{4,0,3,2,1:T(8,128)S(1)} %fusion.65, f32[64,64]{1,0:T(8,128)S(1)} %get-tuple-element.29, f32[64,64]{1,0:T(8,128)S(1)} %fusion.88, ...), kind=kOutput, calls=%fused_computation.21 | convolution fusion | flops 1612759040 | bytes 12632064 | tf_op jit(solution)/shard_map/dot_general | solution.py:191
  309.9 2.0 copy.33
  311.9 5.1 %all-to-all-start.3 = ((f32[16,4,64,128]{3,2,1,0:T(8,128)}), f32[16,4,64,128]{3,2,1,0:T(8,128)}, u32[]{:S(2)}, u32[]{:S(2)}) async-start(f32[16,4,64,128]{3,2,1,0:T(8,128)} %copy.33), calls=%async_computation.3 | async-start | bytes 4194304 | tf_op jit(solution)/shard_map/all_to_all | solution.py:194
  317.0 4.6 %fusion.17 = f32[16,16]{1,0:T(8,128)S(1)} fusion(f32[16,4,64,128]{3,0,2,1:T(8,128)} %copy-done, f32[16,4,64,128]{3,0,2,1:T(8,128)S(1)} %bitcast.127), kind=kOutput, calls=%fused_computation.36 | convolution fusion | flops 50331648 | bytes 4195328 | tf_op jit(solution)/shard_map/dot_general | solution.py:114
  321.6 2.9 fusion.20
  324.5 3.3 fusion.38
  327.7 2.9 fusion.32
  330.7 61.4 %psum.7 = f32[1,2,16,16]{3,2,1,0:T(8,128)} all-reduce(f32[1,2,16,16]{3,2,1,0:T(8,128)S(1)} %fusion.77), channel_id=1, replica_groups=mesh['path'=2,'mesh'=2,'grid'=8] {'mesh','grid'}, use_global_device_ids=true, to_apply=%region_2.3 | all-reduce | flops 512 | bytes 4096 | tf_op jit(solution)/shard_map/psum | solution.py:195
  392.1 3.2 copy.34
  (38 shorter events, 16.1 us)
Async XLA Ops:
  9.6 12.6 %all-to-all-start = ((f32[1,1,8,64,128]{4,3,1,0,2:T(8,128)}), f32[1,1,8,64,128]{4,3,1,0,2:T(8,128)S(1)}, u32[]{:S(2)}, u32[]{:S(2)}) async-start(f32[1,1,8,64,128]{4,3,1,0,2:T(8,128)} %all_gather.3), calls=%async_computation | async-start | bytes 524288 | tf_op jit(solution)/shard_map/all_to_all | solution.py:152
  61.3 6.7 %copy-start.2 = (s32[2,3]{1,0:T(2,128)S(1)}, s32[2,3]{1,0:T(2,128)}, u32[]{:S(2)}) copy-start(s32[2,3]{1,0:T(2,128)} %param.8) | copy-start | bytes 76
  61.3 6.7 %copy-start.3 = (s32[1,3]{1,0:T(1,128)S(1)}, s32[1,3]{1,0:T(1,128)}, u32[]{:S(2)}) copy-start(s32[1,3]{1,0:T(1,128)} %param.7) | copy-start | bytes 40
  61.3 94.4 %all-to-all-start.1 = ((f32[2,16,4,64,128]{4,2,1,0,3:T(4,128)}), f32[2,16,4,64,128]{4,2,1,0,3:T(4,128)}, u32[]{:S(2)}, u32[]{:S(2)}) async-start(f32[2,16,4,64,128]{4,2,1,0,3:T(4,128)} %copy.24), calls=%async_computation.1 | async-start | bytes 8388608 | tf_op jit(solution)/shard_map/all_to_all | solution.py:178
  308.6 1.3 copy-start
  311.9 80.2 %all-to-all-start.3 = ((f32[16,4,64,128]{3,2,1,0:T(8,128)}), f32[16,4,64,128]{3,2,1,0:T(8,128)}, u32[]{:S(2)}, u32[]{:S(2)}) async-start(f32[16,4,64,128]{3,2,1,0:T(8,128)} %copy.33), calls=%async_computation.3 | async-start | bytes 4194304 | tf_op jit(solution)/shard_map/all_to_all | solution.py:194
  317.0 4.6 %copy-start.1 = (f32[16,4,64,128]{3,0,2,1:T(8,128)S(1)}, f32[16,4,64,128]{3,0,2,1:T(8,128)}, u32[]{:S(2)}) copy-start(f32[16,4,64,128]{3,0,2,1:T(8,128)} %copy-done) | copy-start | bytes 6291460
where the time goes:
time: 400 us; the launch traced here: 396 us
  blocking collectives  172 us (43%)
  waiting for transfers between devices  87 us (22%)
  matrix products  75.3 us (19%)
  local copies, waits for them, and re-layouts  29.8 us (7%)
  other arithmetic  15.3 us (4%)
  starting transfers between devices  15.1 us (4%)
    all_to_all x1, blocking collectives, per_device(): lax.all_to_all(moved, ('mesh', 'grid'), split_axis=2, concat_axis=3, tile...  101 us
    all_to_all x1, waiting for transfers between devices, per_device(): lax.all_to_all(pair_field, ('mesh', 'grid'), split_axis=3, concat_axis=2,...  87 us
    psum x1, blocking collectives, per_device(): intersection = lax.psum(partial_value, ('mesh', 'grid'))  61.4 us
    dot_general x4, matrix products, along_axis(): jnp.einsum(form, values, cosine_table, precision=HIGHEST_PRECISION)  36.5 us
    dot_general x4, matrix products, along_axis(): sin_part = jnp.einsum(form, values, sine_table, precision=HIGHEST_PRECISION)  16.9 us
    all_gather x1, blocking collectives, per_device(): whole_orbitals = lax.all_gather(occupied, 'path', axis=3, tiled=True)  8.98 us
  transfers between devices with their start and end apart: 3, of which 1 were waited for; matrix products, arithmetic and copies ran while one was open for 6% of the time, Pallas kernels for 0%

commit v1 on v0

--- a/solution.py
+++ b/solution.py
@@ -184,7 +184,15 @@
         * kernel[:, None]
     )
     moved = along_axis(moved, cos_x.T, sin_x.T, 2, True)
-    potential = lax.all_to_all(moved, ("mesh", "grid"), split_axis=2, concat_axis=3, tiled=True)
+    potential = jnp.concatenate(
+        lax.all_to_all(
+            jnp.stack(jnp.split(moved, lax.axis_size(("mesh", "grid")), axis=2)),
+            ("mesh", "grid"),
+            0,
+            0,
+        ),
+        axis=3,
+    )
     values = potential
     values = along_axis(values, cos_y, sin_y, 3, True)
     applied = accumulate(

time: 400 us -> 402 us (level)
  no operation moved by 1% of the time
where the time goes in v1:
time: 402 us; the launch traced here: 397 us
  blocking collectives  172 us (43%)
  waiting for transfers between devices  87 us (22%)
  matrix products  77.9 us (19%)
  local copies, waits for them, and re-layouts  28.4 us (7%)
  other arithmetic  15.5 us (4%)
  starting transfers between devices  15.1 us (4%)
    all_to_all x1, blocking collectives, per_device(): lax.all_to_all(jnp.stack(jnp.split(moved, lax.axis_size(('mesh', 'grid'))...  101 us
    all_to_all x1, waiting for transfers between devices, per_device(): lax.all_to_all(pair_field, ('mesh', 'grid'), split_axis=3, concat_axis=2,...  87 us
    psum x1, blocking collectives, per_device(): intersection = lax.psum(partial_value, ('mesh', 'grid'))  61.4 us
    dot_general x4, matrix products, along_axis(): jnp.einsum(form, values, cosine_table, precision=HIGHEST_PRECISION)  37.9 us
    dot_general x4, matrix products, along_axis(): sin_part = jnp.einsum(form, values, sine_table, precision=HIGHEST_PRECISION)  18.4 us
    all_gather x1, blocking collectives, per_device(): whole_orbitals = lax.all_gather(occupied, 'path', axis=3, tiled=True)  8.98 us
  transfers between devices with their start and end apart: 3, of which 1 were waited for; matrix products, arithmetic and copies ran while one was open for 6% of the time, Pallas kernels for 0%

profile of v1, /device:TPU:0, one launch (start us, length us, event | category | flops | bytes accessed | tf_op | source)
XLA Modules:
  0.0 397.3 jit_solution(11691640065967811814)
XLA Ops:
  0.6 9.0 %all_gather.3 = f32[1,1,8,64,128]{4,3,1,0,2:T(8,128)} all-gather(f32[1,1,8,32,128]{4,3,1,0,2:T(8,128)} %bitcast.196), channel_id=1, replica_groups=mesh['path'=2,'mesh'=2,'grid'=8] {'path'}, dimensions={3}, use_global_device_ids=true | all-gather | bytes 393216 | tf_op jit(solution)/shard_map/all_gather | solution.py:145
  9.6 3.4 all-to-all-start
  14.1 1.7 constant_dynamic-slice_fusion
  18.1 2.0 copy.31
  20.1 2.0 copy.32
  23.9 3.4 multiply_add_fusion
  27.3 4.0 %fusion = f32[2,16,4,64,128]{4,3,2,1,0:T(8,128)S(1)} fusion(f32[2,1,16,4,64,64]{5,4,3,2,0,1:T(8,128)S(1)} %get-tuple-element.11, f32[2,1,16,4,64,64]{5,4,3,2,0,1:T(8,128)S(1)} %get-tuple-element.10, f32[64,64]{1,0:T(8,128)S(1)} %get-tuple-element.29, f32[64,64]{1,0:T(8,128)S(1)} %get-tuple-element.28, f32[64,64]{1,0:T(8,128)S(1)} %fusion.110), kind=kOutput, calls=%fused_computation.5 | convolution fusion | flops 1611710464 | bytes 8437760 | tf_op jit(solution)/shard_map/dot_general | solution.py:161
  31.3 4.2 %convolution_bitcast_fusion.2 = f32[2,16,4,64,128]{4,3,2,1,0:T(8,128)S(1)} fusion(f32[2,16,4,64,128]{4,3,2,1,0:T(8,128)S(1)} %fusion), kind=kOutput, calls=%fused_computation.29 | convolution fusion | flops 805363712 | bytes 8388608 | tf_op jit(solution)/shard_map/abcde,dw->abcwe/dot_general | solution.py:48
  35.5 1.9 fusion.161
  37.4 19.3 %maximum_add_fusion = f32[2,16,4,64,128]{4,3,2,1,0:T(8,128)S(1)} fusion(f32[2,16,4,64,64]{4,3,2,1,0:T(8,128)S(1)} %get-tuple-element.19, f32[2,16,4,64,64]{4,3,2,1,0:T(8,128)S(1)} %get-tuple-element.18, f32[2,16,4,64,128]{4,3,2,1,0:T(8,128)S(1)} %fusion), kind=kOutput, calls=%fused_computation.8 | convolution fusion | flops 807460864 | bytes 12582912 | tf_op jit(solution)/shard_map/abcde,dw->abcwe/dot_general | solution.py:47
  56.6 4.7 %copy.35 = f32[2,16,4,64,128]{4,2,1,0,3:T(4,128)} copy(f32[2,16,4,64,128]{4,3,2,1,0:T(8,128)S(1)} %maximum_add_fusion) | data formatting | bytes 8388608 | tf_op jit(solution)/shard_map/add | solution.py:54
  61.3 6.6 %all-to-all-start.1 = ((f32[2,16,4,64,128]{4,2,1,0,3:T(4,128)}), f32[2,16,4,64,128]{4,2,1,0,3:T(4,128)}, u32[]{:S(2)}, u32[]{:S(2)}) async-start(f32[2,16,4,64,128]{4,2,1,0,3:T(4,128)} %copy.35), calls=%async_computation.1 | async-start | bytes 8388608 | tf_op jit(solution)/shard_map/all_to_all | solution.py:178
  68.7 87.0 %all-to-all-done.1 = f32[2,16,4,64,128]{4,2,1,0,3:T(4,128)} async-done(((f32[2,16,4,64,128]{4,2,1,0,3:T(4,128)}), f32[2,16,4,64,128]{4,2,1,0,3:T(4,128)}, u32[]{:S(2)}, u32[]{:S(2)}) %all-to-all-start.1) | async-done | bytes 4194336 | tf_op jit(solution)/shard_map/all_to_all | solution.py:178
  155.7 3.4 copy.36
  159.1 4.2 %convolution_bitcast_fusion.1 = f32[2,16,64,4,128]{4,2,3,1,0:T(8,128)S(1)} fusion(f32[2,16,64,4,128]{4,2,3,1,0:T(8,128)S(1)} %bitcast.189, s32[64]{0:T(128)S(1)} %fusion.113), kind=kOutput, calls=%fused_computation.28 | convolution fusion | flops 805363712 | bytes 8388864 | tf_op jit(solution)/shard_map/abcde,cw->abwde/dot_general | solution.py:48
  163.3 1.9 fusion.160
  165.2 6.8 %fusion.3 = f32[2,16,64,4,128]{4,2,3,1,0:T(8,128)S(1)} fusion(f32[2,16,64,4,64]{4,2,3,1,0:T(8,128)S(1)} %get-tuple-element.17, f32[2,16,64,4,64]{4,2,3,1,0:T(8,128)S(1)} %get-tuple-element.16, f32[2,16,64,4,128]{4,2,3,1,0:T(8,128)S(1)} %bitcast.190, f32[2,64,4,128]{3,1,2,0:T(8,128)S(1)} %pad_maximum_fusion, s32[64]{0:T(128)S(1)} %fusion.113), kind=kOutput, calls=%fused_computation.10 | convolution fusion | flops 808509440 | bytes 12845312 | tf_op jit(solution)/shard_map/abcde,cw->abwde/dot_general | solution.py:47
  172.0 4.3 %convolution_bitcast_fusion = f32[2,16,64,4,128]{4,2,3,1,0:T(8,128)S(1)} fusion(f32[2,16,64,4,128]{4,2,3,1,0:T(8,128)S(1)} %fusion.3, s32[64]{0:T(128)S(1)} %fusion.113), kind=kOutput, calls=%fused_computation.27 | convolution fusion | flops 805363712 | bytes 8388864 | tf_op jit(solution)/shard_map/abcde,cw->abwde/dot_general | solution.py:48
  178.0 6.2 %maximum_add_fusion.2 = f32[2,16,64,4,128]{4,2,3,1,0:T(8,128)S(1)} fusion(f32[2,16,64,4,64]{4,2,3,1,0:T(8,128)S(1)} %get-tuple-element.15, f32[2,16,64,4,64]{4,2,3,1,0:T(8,128)S(1)} %get-tuple-element.14, f32[2,16,64,4,128]{4,2,3,1,0:T(8,128)S(1)} %fusion.3, s32[64]{0:T(128)S(1)} %fusion.113), kind=kOutput, calls=%fused_computation.11 | convolution fusion | flops 807460864 | bytes 12583168 | tf_op jit(solution)/shard_map/abcde,cw->abwde/dot_general | solution.py:47
  185.7 101.4 %all_to_all.50 = f32[16,2,16,4,4,128]{5,3,4,2,1,0:T(4,128)S(1)} all-to-all(f32[16,2,16,4,4,128]{5,3,4,2,1,0:T(4,128)S(1)} %fusion.51), channel_id=1, replica_groups=mesh['path'=2,'mesh'=2,'grid'=8] {'mesh','grid'}, dimensions={0} | all-to-all | bytes 8388608 | tf_op jit(solution)/shard_map/all_to_all | solution.py:188
  288.4 5.7 %fusion.12 = f32[2,16,4,64,128]{4,3,2,1,0:T(8,128)S(1)} fusion(f32[2,16,4,64,128]{4,1,3,2,0:T(8,128)S(1)} %bitcast.191), kind=kOutput, calls=%fused_computation.25 | convolution fusion | flops 805363712 | bytes 8388608 | tf_op jit(solution)/shard_map/abcde,dw->abcwe/dot_general | solution.py:48
  294.1 5.7 %fusion.10 = f32[64,2,16,4,128]{4,0,3,2,1:T(8,128)S(1)} fusion(f32[2,16,4,64,128]{4,1,3,2,0:T(8,128)S(1)} %bitcast.192), kind=kOutput, calls=%fused_computation.23 | convolution fusion | flops 805363712 | bytes 8388608 | tf_op jit(solution)/shard_map/abcde,dw->abcwe/dot_general | solution.py:47
  299.8 1.9 slice_negate_fusion
  301.7 4.0 %fusion.15 = f32[2,1,16,4,64,128]{5,4,3,2,0,1:T(8,128)S(1)} fusion(f32[2,16,4,64,64]{4,3,2,1,0:T(8,128)S(1)} %get-tuple-element.13, f32[2,16,4,64,64]{4,3,2,1,0:T(8,128)S(1)} %get-tuple-element.12, f32[64,2,16,4,128]{4,0,3,2,1:T(8,128)S(1)} %fusion.10, f32[64,64]{1,0:T(8,128)S(1)} %get-tuple-element.29, f32[64,64]{1,0:T(8,128)S(1)} %fusion.110, ...), kind=kOutput, calls=%fused_computation.26 | convolution fusion | flops 1612759040 | bytes 12632064 | tf_op jit(solution)/shard_map/dot_general | solution.py:199
  311.5 2.0 copy.46
  313.5 5.1 %all-to-all-start.3 = ((f32[16,4,64,128]{3,2,1,0:T(8,128)}), f32[16,4,64,128]{3,2,1,0:T(8,128)}, u32[]{:S(2)}, u32[]{:S(2)}) async-start(f32[16,4,64,128]{3,2,1,0:T(8,128)} %copy.46), calls=%async_computation.3 | async-start | bytes 4194304 | tf_op jit(solution)/shard_map/all_to_all | solution.py:202
  318.6 4.6 %fusion.24 = f32[16,16]{1,0:T(8,128)S(1)} fusion(f32[16,4,64,128]{3,0,2,1:T(8,128)} %copy-done, f32[16,4,64,128]{3,0,2,1:T(8,128)S(1)} %bitcast.185), kind=kOutput, calls=%fused_computation.40 | convolution fusion | flops 50331648 | bytes 4195328 | tf_op jit(solution)/shard_map/dot_general | solution.py:114
  323.2 2.9 fusion.27
  326.0 3.3 fusion.45
  329.3 2.9 fusion.39
  332.2 61.4 %psum.7 = f32[1,2,16,16]{3,2,1,0:T(8,128)} all-reduce(f32[1,2,16,16]{3,2,1,0:T(8,128)S(1)} %fusion.99), channel_id=1, replica_groups=mesh['path'=2,'mesh'=2,'grid'=8] {'mesh','grid'}, use_global_device_ids=true, to_apply=%region_2.3 | all-reduce | flops 512 | bytes 4096 | tf_op jit(solution)/shard_map/psum | solution.py:203
  393.7 3.2 copy.47
  (53 shorter events, 15.9 us)
Async XLA Ops:
  9.6 12.6 %all-to-all-start = ((f32[1,1,8,64,128]{4,3,1,0,2:T(8,128)}), f32[1,1,8,64,128]{4,3,1,0,2:T(8,128)S(1)}, u32[]{:S(2)}, u32[]{:S(2)}) async-start(f32[1,1,8,64,128]{4,3,1,0,2:T(8,128)} %all_gather.3), calls=%async_computation | async-start | bytes 524288 | tf_op jit(solution)/shard_map/all_to_all | solution.py:152
  61.3 6.7 %copy-start.2 = (s32[2,3]{1,0:T(2,128)S(1)}, s32[2,3]{1,0:T(2,128)}, u32[]{:S(2)}) copy-start(s32[2,3]{1,0:T(2,128)} %param.8) | copy-start | bytes 76
  61.3 6.7 %copy-start.3 = (s32[1,3]{1,0:T(1,128)S(1)}, s32[1,3]{1,0:T(1,128)}, u32[]{:S(2)}) copy-start(s32[1,3]{1,0:T(1,128)} %param.7) | copy-start | bytes 40
  61.3 94.4 %all-to-all-start.1 = ((f32[2,16,4,64,128]{4,2,1,0,3:T(4,128)}), f32[2,16,4,64,128]{4,2,1,0,3:T(4,128)}, u32[]{:S(2)}, u32[]{:S(2)}) async-start(f32[2,16,4,64,128]{4,2,1,0,3:T(4,128)} %copy.35), calls=%async_computation.1 | async-start | bytes 8388608 | tf_op jit(solution)/shard_map/all_to_all | solution.py:178
  310.2 1.3 copy-start
  313.5 80.2 %all-to-all-start.3 = ((f32[16,4,64,128]{3,2,1,0:T(8,128)}), f32[16,4,64,128]{3,2,1,0:T(8,128)}, u32[]{:S(2)}, u32[]{:S(2)}) async-start(f32[16,4,64,128]{3,2,1,0:T(8,128)} %copy.46), calls=%async_computation.3 | async-start | bytes 4194304 | tf_op jit(solution)/shard_map/all_to_all | solution.py:202
  318.5 4.6 %copy-start.1 = (f32[16,4,64,128]{3,0,2,1:T(8,128)S(1)}, f32[16,4,64,128]{3,0,2,1:T(8,128)}, u32[]{:S(2)}) copy-start(f32[16,4,64,128]{3,0,2,1:T(8,128)} %copy-done) | copy-start | bytes 6291460
